TPU v7x, 32 devices: a whole 2x2x4 slice. The times are simulated.
32 devices in a mesh: rep: 4 (over y, core), shard: 8 (over z, x).
Axes of the slice: x: 2, y: 2, z: 4, core: 2. Of those that a mesh axis runs over, the one named last changes fastest.
Arguments:
- weights: bfloat16 [4, 4096, 5120], P('rep', 'shard'), may hold values from -12 to 12
- warm_start: bfloat16 [4, 2, 16, 5120], P('rep'), may hold values from -4 to 4, as said below
Outputs:
- corrected: bfloat16 [4, 4096, 5120], P('rep', 'shard')
- factors: float32 [4, 2, 16, 5120], P('rep')
Inputs may be any that keep to these rules, and one draw needn't show every extreme that they name: `warm_start`: replicas whose indices differ only in bit 0 hold equal start vectors for matching 0, and replicas whose indices differ by 2 hold equal start vectors for matching 1.
All inputs are finite; a program needn't handle non-finite values.
Results may differ from a plain program's by a relative error of at most 0.0049.
Values sent between devices are 32-bit elements; how exact they have to be, the bound alone decides.
A program may use at most 64 MiB of HBM per device.

v0:
```python
import jax
import jax.numpy as jnp
from jax import lax
from jax.sharding import PartitionSpec as P

STEPS = 2


def partner(value, axis, stride):
    return lax.ppermute(value, axis, [(i, i ^ 1 << stride) for i in range(lax.axis_size(axis))])


def shards(weights, warm_start):
    current = weights[0]
    replica = lax.axis_index("rep")
    half_rep = lax.axis_size("rep") // 2
    top_bit = lax.axis_size("rep").bit_length() - 2
    factor_list = []
    for matching in range(STEPS):
        if matching == 0:
            bit_number = 0
            parity = 1.0 - 2.0 * (replica % 2).astype(jnp.float32)
        else:
            bit_number = top_bit
            parity = 1.0 - 2.0 * (replica // half_rep).astype(jnp.float32)
        starts = warm_start[0, matching]
        sketch = lax.dot_general(
            starts, current, (((1,), (1,)), ((), ())), preferred_element_type=jnp.float32
        )
        sketch_other = partner(sketch, "rep", bit_number)
        differ = parity * (sketch - sketch_other)
        gram_local = lax.dot_general(
            differ, differ, (((1,), (1,)), ((), ())), precision=lax.Precision.HIGHEST
        )
        gram_sum = lax.psum(gram_local, "shard")
        triangle = jnp.linalg.cholesky(gram_sum)
        basis_rows = lax.linalg.triangular_solve(triangle, differ, left_side=True, lower=True)
        signed = parity * jnp.dot(
            basis_rows.astype(jnp.bfloat16), current, preferred_element_type=jnp.float32
        )
        summed = lax.psum(signed, "shard")
        factors = summed + partner(summed, "rep", bit_number)
        change = lax.dot_general(
            basis_rows, factors, (((0,), (0,)), ((), ())), precision=lax.Precision.HIGHEST
        )
        current = (current.astype(jnp.float32) - 0.5 * parity * change).astype(jnp.bfloat16)
        factor_list.append(factors)
    return (current[None], jnp.stack(factor_list)[None])


def solution(mesh):
    placed = (P("rep", "shard", None), P("rep", None, None, None))
    return jax.shard_map(
        shards,
        mesh=mesh,
        in_specs=placed,
        out_specs=(P("rep", "shard", None), P("rep", None, None, None)),
        check_vma=False,
    )
```

profile of v0, /device:TPU:0, one launch (start us, length us, event | category | flops | bytes accessed | tf_op | source)
XLA Modules:
  0.0 259.3 jit_solution(16875092373942699540)
XLA Ops:
  7.2 4.0 %fusion.2 = f32[16,512]{1,0:T(8,128)S(1)} fusion(bf16[1,512,5120]{2,1,0:T(8,128)(2,1)} %param.5, bf16[1,2,16,5120]{3,2,1,0:T(8,128)(2,1)} %param.6), kind=kOutput, calls=%fused_computation.6 | convolution fusion | flops 83886080 | bytes 5439488 | tf_op jit(solution)/shard_map/dot_general | solution.py:27
  11.7 0.9 collective-permute-done
  12.7 23.2 %psum.28 = f32[16,16]{0,1:T(8,128)S(1)} all-reduce(f32[16,16]{0,1:T(8,128)S(1)} %fusion.13), channel_id=1, replica_groups=mesh['rep'=4,'shard'=8] {'shard'}, use_global_device_ids=true, to_apply=%region_0.1 | all-reduce | flops 256 | bytes 2048 | tf_op jit(solution)/shard_map/psum | solution.py:35
  36.1 1.5 cholesky.44
  38.2 0.6 fusion.16
  38.9 1.2 custom-call.6
  40.3 4.0 %convolution_multiply_fusion.1 = f32[16,5120]{1,0:T(8,128)} fusion(bf16[1,512,5120]{2,1,0:T(8,128)(2,1)} %param.5, f32[]{:T(128)S(6)} %sub.22, f32[16,512]{1,0:T(8,128)S(1)} %fusion.12), kind=kOutput, calls=%fused_computation.4 | convolution fusion | flops 83976192 | bytes 5603332 | tf_op jit(solution)/shard_map/dot_general | solution.py:38
  44.4 68.8 %all-reduce.3.cloned.1.call-done = f32[16,5120]{1,0:T(8,128)} async-done(((f32[16,5120]{1,0:T(8,128)}), f32[16,5120]{1,0:T(8,128)}) %all-reduce.3.cloned.1.call-update) | async-done | bytes 327696 | tf_op jit(solution)/shard_map/psum | solution.py:41
  113.2 1.8 collective-permute-done.1
  115.0 10.8 %subtract_convert_fusion.1 = bf16[512,5120]{1,0:T(8,128)(2,1)S(1)} fusion(f32[16,512]{1,0:T(8,128)S(1)} %fusion.12, bf16[1,512,5120]{2,1,0:T(8,128)(2,1)} %param.5, f32[]{:T(128)S(6)} %mul.49, f32[16,5120]{1,0:T(8,128)} %all-reduce.3.cloned.1.call-done, f32[16,5120]{1,0:T(8,128)S(1)} %collective-permute-done.1), kind=kOutput, calls=%fused_computation.1 | convolution fusion | flops 513884160 | bytes 11173892 | tf_op jit(solution)/shard_map/dot_general | solution.py:43
  125.9 2.3 copy-done
  128.2 1.5 convolution_bitcast_fusion
  129.7 1.5 collective-permute-start.2
  131.2 2.4 collective-permute-done.2
  133.8 19.9 %psum.30 = f32[16,16]{0,1:T(8,128)S(1)} all-reduce(f32[16,16]{0,1:T(8,128)S(1)} %fusion.15), channel_id=1, replica_groups=mesh['rep'=4,'shard'=8] {'shard'}, use_global_device_ids=true, to_apply=%region_4.7 | all-reduce | flops 256 | bytes 2048 | tf_op jit(solution)/shard_map/psum | solution.py:35
  153.7 1.5 cholesky.55
  156.5 1.2 custom-call.7
  158.0 4.0 %convolution_multiply_fusion = f32[16,5120]{1,0:T(8,128)} fusion(bf16[512,5120]{1,0:T(8,128)(2,1)} %copy-done, f32[]{:T(128)S(6)} %sub.26, f32[16,512]{1,0:T(8,128)S(1)} %fusion.14), kind=kOutput, calls=%fused_computation.3 | convolution fusion | flops 83976192 | bytes 5603332 | tf_op jit(solution)/shard_map/dot_general | solution.py:38
  162.0 68.8 %all-reduce.5.cloned.1.call-done = f32[16,5120]{1,0:T(8,128)} async-done(((f32[16,5120]{1,0:T(8,128)}), f32[16,5120]{1,0:T(8,128)}) %all-reduce.5.cloned.1.call-update) | async-done | bytes 327696 | tf_op jit(solution)/shard_map/psum | solution.py:41
  230.8 1.5 collective-permute-start.3
  232.3 6.3 %collective-permute-done.3 = f32[16,5120]{1,0:T(8,128)S(1)} collective-permute-done((f32[16,5120]{1,0:T(8,128)}, f32[16,5120]{1,0:T(8,128)S(1)}, u32[]{:S(2)}, u32[]{:S(2)}) %collective-permute-start.3) | collective-permute-done | bytes 327712 | tf_op jit(solution)/shard_map/ppermute | solution.py:10
  238.6 1.0 add_bitcast_fusion
  239.6 0.9 maximum_bitcast_fusion
  240.5 11.9 %fusion = bf16[1,512,5120]{2,1,0:T(8,128)(2,1)} fusion(f32[16,512]{1,0:T(8,128)S(1)} %fusion.14, bf16[512,5120]{1,0:T(8,128)(2,1)} %copy-done, f32[]{:T(128)S(6)} %mul.57, f32[16,5120]{1,0:T(8,128)} %all-reduce.5.cloned.1.call-done, f32[16,5120]{1,0:T(8,128)S(1)} %collective-permute-done.3), kind=kOutput, calls=%fused_computation.2 | convolution fusion | flops 513884160 | bytes 11173892 | tf_op jit(solution)/shard_map/dot_general | solution.py:43
  (25 shorter events, 3.6 us)
Async XLA Ops:
  7.2 106.0 %all-reduce.3.cloned.1.call-start = ((), (), s32[]{:S(2)}) async-start(), calls=%async_computation | async-start | bytes 655360 | tf_op jit(solution)/shard_map/psum | solution.py:41
  11.2 1.4 collective-permute-start
  44.4 186.4 %all-reduce.5.cloned.1.call-start = ((), (), s32[]{:S(2)}) async-start(), calls=%async_computation.1 | async-start | bytes 655360 | tf_op jit(solution)/shard_map/psum | solution.py:41
  113.2 1.8 collective-permute-start.1
  113.2 15.0 %copy-start.2 = (bf16[1,2,16,5120]{3,2,1,0:T(8,128)(2,1)S(1)}, bf16[1,2,16,5120]{3,2,1,0:T(8,128)(2,1)}, u32[]{:S(2)}) copy-start(bf16[1,2,16,5120]{3,2,1,0:T(8,128)(2,1)} %param.6) | copy-start | bytes 983044
  125.9 2.4 copy-start
  128.2 104.0 %copy-start.1 = (f32[16,5120]{1,0:T(8,128)S(1)}, f32[16,5120]{1,0:T(8,128)}, u32[]{:S(2)}) copy-start(f32[16,5120]{1,0:T(8,128)} %all-reduce.3.cloned.1.call-done) | copy-start | bytes 983044
  129.7 3.9 %collective-permute-start.2 = (f32[16,512]{1,0:T(8,128)S(1)}, f32[16,512]{1,0:T(8,128)S(1)}, u32[]{:S(2)}, u32[]{:S(2)}) collective-permute-start(f32[16,512]{1,0:T(8,128)S(1)} %convolution_bitcast_fusion), channel_id=1, source_target_pairs={{0,16},{8,24},{16,0},{24,8},{1,17},{9,25},{17,1},{25,9},{2,18},{10... | collective-permute-start | bytes 98312 | tf_op jit(solution)/shard_map/ppermute | solution.py:10
  230.8 7.8 %collective-permute-start.3 = (f32[16,5120]{1,0:T(8,128)}, f32[16,5120]{1,0:T(8,128)S(1)}, u32[]{:S(2)}, u32[]{:S(2)}) collective-permute-start(f32[16,5120]{1,0:T(8,128)} %all-reduce.5.cloned.1.call-done), channel_id=1, source_target_pairs={{0,16},{8,24},{16,0},{24,8},{1,17},{9,25},{17,1},{25,9},{2,18},{10... | collective-permute-start | bytes 983048 | tf_op jit(solution)/shard_map/ppermute | solution.py:10
Sparse Core Ops, SparseCore 0:
  44.5 68.6 all-reduce.2
  162.2 68.5 all-reduce.4
where the time goes:
time: 260 us; the launch traced here: 259 us
  waiting for transfers between devices  149 us (57%)
  blocking collectives  43.1 us (17%)
  matrix products  37 us (14%)
  between operations  14.1 us (5%)
  other arithmetic  9.97 us (4%)
  starting transfers between devices  3.53 us (1%)
    psum x2, waiting for transfers between devices, shards(): summed = lax.psum(signed, 'shard')  138 us
    psum x2, blocking collectives, shards(): gram_sum = lax.psum(gram_local, 'shard')  43.1 us
    dot_general x2, matrix products, shards(): lax.dot_general(basis_rows, factors, (((0,), (0,)), ((), ())), precision=...  22.7 us
    ppermute x4, waiting for transfers between devices, partner(): lax.ppermute(value, axis, [(i, i ^ 1 << stride) for i in range(lax.axis_s...  11.5 us
    dot_general x2, matrix products, shards(): jnp.dot(basis_rows.astype(jnp.bfloat16), current, preferred_element_type=...  8.02 us
    dot_general x2, matrix products, shards(): lax.dot_general(starts, current, (((1,), (1,)), ((), ())), preferred_elem...  5.49 us
  transfers between devices with their start and end apart: 6, of which 6 were waited for; matrix products, arithmetic and copies ran while one was open for 0% of the time, Pallas kernels for 0%

commit v1 on v0

v1 whole, which is shorter than its diff:
```python
import functools
import math

import jax
import jax.numpy as jnp
from jax import lax
from jax.experimental import pallas as pl
from jax.experimental.pallas import tpu as pltpu
from jax.sharding import PartitionSpec as P

STEPS = 2
LANES = 128
F32 = jnp.float32
BF16 = jnp.bfloat16
NT = (((1,), (1,)), ((), ()))


def split(value):
    high = value.astype(BF16).astype(F32)
    return high, value - high


def stack_left(basis, scale):
    high, low = split(scale * basis)
    rank, rows = basis.shape
    pad = jnp.zeros((LANES - 3 * rank, rows), F32)
    return jnp.concatenate([high, high, low, pad], axis=0).T.astype(BF16)


def stack_right(factor):
    high, low = split(factor)
    rank, cols = factor.shape
    pad = jnp.zeros((LANES - 3 * rank, cols), F32)
    return jnp.concatenate([high, low, high, pad], axis=0).astype(BF16)


def whiten(gram, differ):
    rank = differ.shape[0]
    row = lax.broadcasted_iota(jnp.int32, (rank, 1), 0)
    pivots = jnp.ones((rank, 1), F32)
    for k in range(rank):
        pivot = gram[k : k + 1, k : k + 1]
        pivots = jnp.where(row == k, pivot, pivots)
        if k == rank - 1:
            break
        column = jnp.where(row > k, gram[:, k : k + 1] / pivot, 0.0)
        gram = gram - column * gram[k : k + 1, :]
        differ = differ - column * differ[k : k + 1, :]
    return differ / jnp.sqrt(pivots)


def comm_kernel(
    nrep, nsh, nown,
    w_hbm, starts, cur_out, fac_out, bt_out,
    cur, sk, skin, gbuf, pbuf, pin, psum, rsbuf, fac, bt,
    ld_sem, st_sem, fo_sem, sk_s, sk_r, g_s, g_r, p_s, p_r, rs_s, rs_r, ag_s, ag_r, fw_s, fw_r,
):
    rows, cols = cur.shape
    rank = starts.shape[1]
    half_rank = rank // 2
    width = cols // nown
    stride = nsh // nown
    half = nrep // 2
    me_r = lax.axis_index("rep")
    me_s = lax.axis_index("shard")
    me_j = me_s // stride
    bits = (me_r % 2, me_r // half)
    partners = (me_r + 1 - 2 * (me_r % 2), (me_r + half) % nrep)
    signs = tuple((1 - 2 * b).astype(F32) for b in bits)

    def where(j):
        return pl.ds(pl.multiple_of(j * width, LANES), width)

    def load(c):
        return pltpu.make_async_copy(
            w_hbm.at[:, pl.ds(c * width, width)], cur.at[:, pl.ds(c * width, width)], ld_sem.at[c]
        )

    def remote(src, dst, ssem, rsem, rep, shard):
        return pltpu.make_async_remote_copy(
            src_ref=src, dst_ref=dst, send_sem=ssem, recv_sem=rsem,
            device_id={"rep": rep, "shard": shard}, device_id_type=pl.DeviceIdType.MESH,
        )

    def owner(fn, negate=False):
        if stride == 1:
            if not negate:
                fn()
        else:
            here = me_s % stride != 0 if negate else me_s % stride == 0
            pl.when(here)(fn)

    for c in range(nown):
        load(c).start()

    barrier = pltpu.get_barrier_semaphore()
    for o in range(1, nsh):
        pl.semaphore_signal(
            barrier, inc=1, device_id={"rep": me_r, "shard": (me_s + o) % nsh},
            device_id_type=pl.DeviceIdType.MESH,
        )
    for p in partners:
        pl.semaphore_signal(
            barrier, inc=1, device_id={"rep": p, "shard": me_s},
            device_id_type=pl.DeviceIdType.MESH,
        )

    sketch = jnp.zeros((rank, rows), F32)
    for c in range(nown):
        load(c).wait()
        part = pl.ds(c * width, width)
        sketch = sketch + lax.dot_general(
            starts[0, :, part], cur[:, part], NT, preferred_element_type=F32
        )
    pl.semaphore_wait(barrier, nsh - 1 + 2)

    for k in range(STEPS):
        bit, mate, sign = bits[k], partners[k], signs[k]
        sk[k] = sketch
        swap = remote(sk.at[k], skin.at[k], sk_s.at[k], sk_r.at[k], mate, me_s)
        swap.start()
        swap.wait_recv()
        differ = sign * (sketch - skin[k])
        wide = jnp.concatenate([differ, jnp.zeros((LANES - rank, rows), F32)], axis=0)
        gram = lax.dot_general(
            differ, wide, NT, precision=lax.Precision.HIGHEST, preferred_element_type=F32
        )
        gbuf[k, me_s] = gram[:half_rank] + pltpu.roll(gram[half_rank:], rank, 1)

        def gsend(o):
            other = (me_s + o) % nsh
            return remote(
                gbuf.at[k, me_s], gbuf.at[k, me_s], g_s.at[k, other], g_r.at[k, me_s], me_r, other
            )

        def gwait(o):
            other = (me_s + o) % nsh
            return remote(
                gbuf.at[k, other], gbuf.at[k, other], g_s.at[k, other], g_r.at[k, other], me_r, other
            )

        for o in range(1, nsh):
            gsend(o).start()
        for o in range(1, nsh):
            gwait(o).wait_recv()
        total = gbuf[k, 0]
        for s in range(1, nsh):
            total = total + gbuf[k, s]
        gram = jnp.concatenate([total, pltpu.roll(total, LANES - rank, 1)], axis=0)
        basis = whiten(gram, differ)
        basis_half = basis.astype(BF16)

        def psend(j):
            return remote(
                pbuf.at[k, 1 - bit, :, where(j)], pin.at[k, j], p_s.at[k, j], p_r.at[k, j], mate, me_s
            )

        def rsend(j):
            return remote(
                psum.at[k, j], rsbuf.at[k, me_s], rs_s.at[k, j], rs_r.at[k, me_s], me_r, j * stride
            )

        def rwait(o):
            other = (me_s + o) % nsh
            return remote(
                rsbuf.at[k, other], rsbuf.at[k, other], rs_s.at[k, 0], rs_r.at[k, other], me_r, other
            )

        def asend(o):
            other = (me_s + o) % nsh
            piece = fac.at[k, bit, :, where(me_j)]
            return remote(piece, piece, ag_s.at[k, other], ag_r.at[k, me_j], me_r, other)

        def await_piece(j):
            piece = fac.at[k, bit, :, where(j)]
            return remote(piece, piece, ag_s.at[k, 0], ag_r.at[k, j], me_r, j * stride)

        def fsend(j):
            piece = fac.at[k, bit, :, where(j)]
            return remote(piece, piece, fw_s.at[k, j], fw_r.at[k, j], mate, me_s)

        def fwait(j):
            piece = fac.at[k, 1 - bit, :, where(j)]
            return remote(piece, piece, fw_s.at[k, j], fw_r.at[k, j], mate, me_s)

        order = [(me_j + 1 + i) % nown for i in range(nown)]

        def pass_on(i):
            j = order[i]
            psend(j).wait_recv()
            psum[k, j] = pbuf[k, bit, :, where(j)] + pin[k, j]
            if i < nown - 1:
                rsend(j).start()
            else:
                owner(lambda: rsend(j).start(), negate=True)

        lag = 2
        for i in range(nown):
            j = order[i]
            product = sign * jnp.dot(
                basis_half, cur[:, where(j)], preferred_element_type=F32
            )
            pbuf[k, 0, :, where(j)] = product[:half_rank]
            pbuf[k, 1, :, where(j)] = product[half_rank:]
            psend(j).start()
            if i >= lag:
                pass_on(i - lag)
        for i in range(max(nown - lag, 0), nown):
            pass_on(i)
        bt[k] = stack_left(basis, -0.5 * sign)

        def reduce_and_send():
            for o in range(1, nsh):
                rwait(o).wait_recv()
            total = psum[k, me_j]
            for o in range(1, nsh):
                total = total + rsbuf[k, (me_s + o) % nsh]
            fac[k, bit, :, where(me_j)] = total
            for o in range(1, nsh):
                asend(o).start()

        owner(reduce_and_send)
        owner(lambda: await_piece(me_j).wait_recv(), negate=True)
        fsend(me_j).start()
        if k + 1 < STEPS:
            sketch = jnp.zeros((rank, rows), F32)

        def take(i, sketch):
            j = (me_j + i) % nown
            fwait(j).wait_recv()
            if k + 1 == STEPS:
                return sketch
            piece = jnp.concatenate([fac[k, 0, :, where(j)], fac[k, 1, :, where(j)]], axis=0)
            change = jnp.dot(bt[k], stack_right(piece), preferred_element_type=F32)
            fresh = (cur[:, where(j)].astype(F32) + change).astype(BF16)
            cur[:, where(j)] = fresh
            pltpu.make_async_copy(
                cur.at[:, where(j)], cur_out.at[:, where(j)], st_sem.at[j]
            ).start()
            return sketch + lax.dot_general(
                starts[k + 1, :, where(j)], fresh, NT, preferred_element_type=F32
            )

        for i in range(1, nown):
            j = (me_j + i) % nown
            await_piece(j).wait_recv()
            fsend(j).start()
            if i >= lag:
                sketch = take(i - lag, sketch)
        for i in range(max(nown - lag, 0), nown):
            sketch = take(i, sketch)

        pltpu.make_async_copy(fac.at[k], fac_out.at[k], fo_sem.at[k]).start()
        swap.wait_send()
        for o in range(1, nsh):
            gsend(o).wait_send()
        for i in range(nown):
            psend(order[i]).wait_send()
            fsend(order[i]).wait_send()
            if i < nown - 1:
                rsend(order[i]).wait_send()
        owner(lambda: rsend(me_j).wait_send(), negate=True)

        def sent_all():
            for o in range(1, nsh):
                asend(o).wait_send()

        owner(sent_all)

    bt_out[...] = bt[STEPS - 1]
    for k in range(STEPS):
        pltpu.make_async_copy(fac.at[k], fac_out.at[k], fo_sem.at[k]).wait()
    for j in range(nown):
        pltpu.make_async_copy(cur.at[:, where(j)], cur_out.at[:, where(j)], st_sem.at[j]).wait()


def update_kernel(cur, bt, fac, out):
    change = jnp.dot(bt[...], stack_right(fac[...]), preferred_element_type=F32)
    out[...] = (cur[...].astype(F32) + change).astype(BF16)


def shards(weights, warm_start):
    nrep, nsh = lax.axis_size("rep"), lax.axis_size("shard")
    _, rows, cols = weights.shape
    rank = warm_start.shape[2]
    half = rank // 2
    nown = math.gcd(cols // LANES, nsh)
    width = cols // nown
    dma = pltpu.SemaphoreType.DMA
    anyspace = pl.BlockSpec(memory_space=pl.ANY)
    vmem = pl.BlockSpec(memory_space=pltpu.VMEM)
    current, factors, bt = pl.pallas_call(
        functools.partial(comm_kernel, nrep, nsh, nown),
        out_shape=(
            jax.ShapeDtypeStruct((rows, cols), BF16),
            jax.ShapeDtypeStruct((STEPS, 2, half, cols), F32),
            jax.ShapeDtypeStruct((rows, LANES), BF16),
        ),
        in_specs=[anyspace, vmem],
        out_specs=(anyspace, anyspace, vmem),
        scratch_shapes=[
            pltpu.VMEM((rows, cols), BF16),
            pltpu.VMEM((STEPS, rank, rows), F32),
            pltpu.VMEM((STEPS, rank, rows), F32),
            pltpu.VMEM((STEPS, nsh, half, LANES), F32),
            pltpu.VMEM((STEPS, 2, half, cols), F32),
            pltpu.VMEM((STEPS, nown, half, width), F32),
            pltpu.VMEM((STEPS, nown, half, width), F32),
            pltpu.VMEM((STEPS, nsh, half, width), F32),
            pltpu.VMEM((STEPS, 2, half, cols), F32),
            pltpu.VMEM((STEPS, rows, LANES), BF16),
            dma((nown,)),
            dma((nown,)),
            dma((STEPS,)),
            dma((STEPS,)),
            dma((STEPS,)),
            dma((STEPS, nsh)),
            dma((STEPS, nsh)),
            dma((STEPS, nown)),
            dma((STEPS, nown)),
            dma((STEPS, nown)),
            dma((STEPS, nsh)),
            dma((STEPS, nsh)),
            dma((STEPS, nown)),
            dma((STEPS, nown)),
            dma((STEPS, nown)),
        ],
        compiler_params=pltpu.CompilerParams(
            collective_id=0, has_side_effects=True, vmem_limit_bytes=48 * 1024 * 1024
        ),
        name="rounds",
    )(weights[0], warm_start[0])
    factors = factors.reshape(STEPS, rank, cols)
    block = pl.BlockSpec((rows, width), lambda c: (0, c))
    corrected = pl.pallas_call(
        update_kernel,
        grid=(nown,),
        out_shape=jax.ShapeDtypeStruct((rows, cols), BF16),
        in_specs=[
            block,
            pl.BlockSpec((rows, LANES), lambda c: (0, 0)),
            pl.BlockSpec((None, rank, width), lambda c: (STEPS - 1, 0, c)),
        ],
        out_specs=block,
        name="update",
    )(current, bt, factors)
    return (corrected[None], factors[None])


def solution(mesh):
    placed = (P("rep", "shard", None), P("rep", None, None, None))
    return jax.shard_map(
        shards,
        mesh=mesh,
        in_specs=placed,
        out_specs=(P("rep", "shard", None), P("rep", None, None, None)),
        check_vma=False,
    )
```

time: 260 us -> 75 us (0.29)
  waiting for transfers between devices: 149 us -> 0 us
  Pallas kernels: 0 us -> 70.8 us
  blocking collectives: 43.1 us -> 0 us
  matrix products: 37 us -> 0 us
  between operations: 14.1 us -> 0.66 us
  other arithmetic: 9.97 us -> 0 us
  starting transfers between devices: 3.53 us -> 0 us
    psum x2 -> x0, waiting for transfers between devices: 138 us -> none  [shards(): summed = lax.psum(signed, 'shard')]
    pallas_call x0 -> x2, Pallas kernels: none -> 70.8 us  [the longest x1 62.5 us: shards(): pl.pallas_call(functools.partial(comm_kernel, nrep, nsh, nown), out_shape...]
    psum x2 -> x0, blocking collectives: 43.1 us -> none  [shards(): gram_sum = lax.psum(gram_local, 'shard')]
    dot_general x8 -> x0, matrix products: 36.5 us -> none  [the longest x2 22.7 us: shards(): lax.dot_general(basis_rows, factors, (((0,), (0,)), ((), ())), precision=...]
    ppermute x4 -> x0, waiting for transfers between devices: 11.5 us -> none  [partner(): lax.ppermute(value, axis, [(i, i ^ 1 << stride) for i in range(lax.axis_s...]
    another operation x12 -> x0, other arithmetic: 9.08 us -> none  [the longest x6 4.26 us: shards(): triangle = jnp.linalg.cholesky(gram_sum)]
    ppermute x4 -> x0, starting transfers between devices: 3.45 us -> none  [partner(): lax.ppermute(value, axis, [(i, i ^ 1 << stride) for i in range(lax.axis_s...]
  transfers between devices with their start and end apart: 6 -> 0, of which waited for: 6 -> 0; matrix products, arithmetic and copies ran while one was open for 0% -> 0% of each run, Pallas kernels for 0% -> 0%
where the time goes in v1:
time: 75 us; the launch traced here: 74.7 us
  Pallas kernels  70.8 us (94%)
  local copies, waits for them, and re-layouts  3.28 us (4%)
    pallas_call x1, Pallas kernels, shards(): pl.pallas_call(functools.partial(comm_kernel, nrep, nsh, nown), out_shape...  62.5 us
    pallas_call x1, Pallas kernels, shards(): pl.pallas_call(update_kernel, grid=(nown,), out_shape=jax.ShapeDtypeStruc...  8.29 us
    unnamed x9, local copies, waits for them, and re-layouts  3.28 us

profile of v1, /device:TPU:0, one launch (start us, length us, event | category | flops | bytes accessed | tf_op | source)
XLA Modules:
  0.0 74.7 jit_solution(989928470343622901)
XLA Ops:
  0.6 0.0 copy-start.2
  0.6 1.0 %copy-done.2 = bf16[1,2,16,5120]{3,2,1,0:T(8,128)(2,1)S(1)} copy-done((bf16[1,2,16,5120]{3,2,1,0:T(8,128)(2,1)S(1)}, bf16[1,2,16,5120]{3,2,1,0:T(8,128)(2,1)}, u32[]{:S(2)}) %copy-start.2) | copy-done | bytes 327704
  1.6 62.5 %rounds.1 = (bf16[512,5120]{1,0:T(8,128)(2,1)}, f32[2,2,8,5120]{3,2,1,0:T(8,128)S(1)}, bf16[512,128]{1,0:T(8,128)(2,1)S(1)}) custom-call(bf16[512,5120]{1,0:T(8,128)(2,1)} %bitcast.8, bf16[2,16,5120]{2,1,0:T(8,128)(2,1)S(1)} %bitcast.7), custom_call_target="tpu_custom_call" | custom-call | tf_op jit(solution)/shard_map/rounds/pallas_call | solution.py:292
  64.1 0.0 copy-start
  64.1 0.8 %copy-done = f32[2,2,8,5120]{3,2,1,0:T(8,128)} copy-done((f32[2,2,8,5120]{3,2,1,0:T(8,128)}, f32[2,2,8,5120]{3,2,1,0:T(8,128)S(1)}, u32[]{:S(2)}) %copy-start) | copy-done | bytes 655384
  64.9 0.0 copy-start.3
  64.9 0.6 copy-done.3
  65.6 0.0 copy-start.1
  65.6 8.3 %update.1 = bf16[512,5120]{1,0:T(8,128)(2,1)} custom-call(bf16[512,5120]{1,0:T(8,128)(2,1)} %get-tuple-element.5.cur, bf16[512,128]{1,0:T(8,128)(2,1)} %copy-done.3, f32[2,16,5120]{2,1,0:T(8,128)} %bitcast.5), custom_call_target="tpu_custom_call" | custom-call | tf_op jit(solution)/shard_map/update/pallas_call | solution.py:335
  73.9 0.0 copy-done.1
  73.9 0.8 %copy.5 = f32[1,2,16,5120]{3,2,1,0:T(8,128)} copy(f32[1,2,16,5120]{3,2,1,0:T(8,128)S(1)} %bitcast.6) | data formatting | bytes 1310720
Async XLA Ops:
  0.6 1.0 %copy-start.2 = (bf16[1,2,16,5120]{3,2,1,0:T(8,128)(2,1)S(1)}, bf16[1,2,16,5120]{3,2,1,0:T(8,128)(2,1)}, u32[]{:S(2)}) copy-start(bf16[1,2,16,5120]{3,2,1,0:T(8,128)(2,1)} %param.3) | copy-start | bytes 983044
  64.1 0.8 %copy-start = (f32[2,2,8,5120]{3,2,1,0:T(8,128)}, f32[2,2,8,5120]{3,2,1,0:T(8,128)S(1)}, u32[]{:S(2)}) copy-start(f32[2,2,8,5120]{3,2,1,0:T(8,128)S(1)} %get-tuple-element.7) | copy-start | bytes 1966084
  64.9 0.6 copy-start.3
  65.6 8.3 %copy-start.1 = (f32[2,2,8,5120]{3,2,1,0:T(8,128)S(1)}, f32[2,2,8,5120]{3,2,1,0:T(8,128)}, u32[]{:S(2)}) copy-start(f32[2,2,8,5120]{3,2,1,0:T(8,128)} %copy-done) | copy-start | bytes 1966084

commit v2 on v1

--- a/solution.py
+++ b/solution.py
@@ -10,6 +10,7 @@
 
 STEPS = 2
 LANES = 128
+VMEM = 67043328
 F32 = jnp.float32
 BF16 = jnp.bfloat16
 NT = (((1,), (1,)), ((), ()))
@@ -51,9 +52,9 @@
 
 def comm_kernel(
     nrep, nsh, nown,
-    w_hbm, starts, cur_out, fac_out, bt_out,
-    cur, sk, skin, gbuf, pbuf, pin, psum, rsbuf, fac, bt,
-    ld_sem, st_sem, fo_sem, sk_s, sk_r, g_s, g_r, p_s, p_r, rs_s, rs_r, ag_s, ag_r, fw_s, fw_r,
+    w_hbm, starts_hbm, cur, fac, bt_out,
+    starts, sk, skin, gbuf, pbuf, pin, psum, rsbuf, bt,
+    ld_sem, wm_sem, sk_s, sk_r, g_s, g_r, p_s, p_r, rs_s, rs_r, ag_s, ag_r, fw_s, fw_r,
 ):
     rows, cols = cur.shape
     rank = starts.shape[1]
@@ -90,6 +91,8 @@
             here = me_s % stride != 0 if negate else me_s % stride == 0
             pl.when(here)(fn)
 
+    warm = pltpu.make_async_copy(starts_hbm, starts, wm_sem)
+    warm.start()
     for c in range(nown):
         load(c).start()
 
@@ -106,6 +109,7 @@
         )
 
     sketch = jnp.zeros((rank, rows), F32)
+    warm.wait()
     for c in range(nown):
         load(c).wait()
         part = pl.ds(c * width, width)
@@ -234,9 +238,6 @@
             change = jnp.dot(bt[k], stack_right(piece), preferred_element_type=F32)
             fresh = (cur[:, where(j)].astype(F32) + change).astype(BF16)
             cur[:, where(j)] = fresh
-            pltpu.make_async_copy(
-                cur.at[:, where(j)], cur_out.at[:, where(j)], st_sem.at[j]
-            ).start()
             return sketch + lax.dot_general(
                 starts[k + 1, :, where(j)], fresh, NT, preferred_element_type=F32
             )
@@ -250,7 +251,6 @@
         for i in range(max(nown - lag, 0), nown):
             sketch = take(i, sketch)
 
-        pltpu.make_async_copy(fac.at[k], fac_out.at[k], fo_sem.at[k]).start()
         swap.wait_send()
         for o in range(1, nsh):
             gsend(o).wait_send()
@@ -268,15 +268,27 @@
         owner(sent_all)
 
     bt_out[...] = bt[STEPS - 1]
-    for k in range(STEPS):
-        pltpu.make_async_copy(fac.at[k], fac_out.at[k], fo_sem.at[k]).wait()
-    for j in range(nown):
-        pltpu.make_async_copy(cur.at[:, where(j)], cur_out.at[:, where(j)], st_sem.at[j]).wait()
-
-
-def update_kernel(cur, bt, fac, out):
-    change = jnp.dot(bt[...], stack_right(fac[...]), preferred_element_type=F32)
-    out[...] = (cur[...].astype(F32) + change).astype(BF16)
+
+
+def update_kernel(cur, bt, fac, cur_out, fac_out, fresh, st_sem, fo_sem):
+    pieces, _, width = fresh.shape
+    factors = pltpu.make_async_copy(fac, fac_out, fo_sem)
+    factors.start()
+
+    def store(c):
+        return pltpu.make_async_copy(
+            fresh.at[c], cur_out.at[:, pl.ds(c * width, width)], st_sem.at[c]
+        )
+
+    for c in range(pieces):
+        part = pl.ds(c * width, width)
+        piece = jnp.concatenate([fac[STEPS - 1, 0, :, part], fac[STEPS - 1, 1, :, part]], axis=0)
+        change = jnp.dot(bt[...], stack_right(piece), preferred_element_type=F32)
+        fresh[c] = (cur[:, part].astype(F32) + change).astype(BF16)
+        store(c).start()
+    factors.wait()
+    for c in range(pieces):
+        store(c).wait()
 
 
 def shards(weights, warm_start):
@@ -287,7 +299,8 @@
     nown = math.gcd(cols // LANES, nsh)
     width = cols // nown
     dma = pltpu.SemaphoreType.DMA
-    anyspace = pl.BlockSpec(memory_space=pl.ANY)
+    held = 2 * rows * cols + 4 * STEPS * rank * cols + 2 * rows * LANES + 13000 * 1024
+    hbm = pl.BlockSpec(memory_space=pltpu.HBM)
     vmem = pl.BlockSpec(memory_space=pltpu.VMEM)
     current, factors, bt = pl.pallas_call(
         functools.partial(comm_kernel, nrep, nsh, nown),
@@ -296,10 +309,10 @@
             jax.ShapeDtypeStruct((STEPS, 2, half, cols), F32),
             jax.ShapeDtypeStruct((rows, LANES), BF16),
         ),
-        in_specs=[anyspace, vmem],
-        out_specs=(anyspace, anyspace, vmem),
+        in_specs=[hbm, hbm],
+        out_specs=(vmem, vmem, vmem),
         scratch_shapes=[
-            pltpu.VMEM((rows, cols), BF16),
+            pltpu.VMEM(warm_start.shape[1:], BF16),
             pltpu.VMEM((STEPS, rank, rows), F32),
             pltpu.VMEM((STEPS, rank, rows), F32),
             pltpu.VMEM((STEPS, nsh, half, LANES), F32),
@@ -307,11 +320,9 @@
             pltpu.VMEM((STEPS, nown, half, width), F32),
             pltpu.VMEM((STEPS, nown, half, width), F32),
             pltpu.VMEM((STEPS, nsh, half, width), F32),
-            pltpu.VMEM((STEPS, 2, half, cols), F32),
             pltpu.VMEM((STEPS, rows, LANES), BF16),
             dma((nown,)),
-            dma((nown,)),
-            dma((STEPS,)),
+            dma,
             dma((STEPS,)),
             dma((STEPS,)),
             dma((STEPS, nsh)),
@@ -326,25 +337,27 @@
             dma((STEPS, nown)),
         ],
         compiler_params=pltpu.CompilerParams(
-            collective_id=0, has_side_effects=True, vmem_limit_bytes=48 * 1024 * 1024
+            collective_id=0, has_side_effects=True, vmem_limit_bytes=VMEM - held
         ),
         name="rounds",
     )(weights[0], warm_start[0])
-    factors = factors.reshape(STEPS, rank, cols)
-    block = pl.BlockSpec((rows, width), lambda c: (0, c))
-    corrected = pl.pallas_call(
+    corrected, factors = pl.pallas_call(
         update_kernel,
-        grid=(nown,),
-        out_shape=jax.ShapeDtypeStruct((rows, cols), BF16),
-        in_specs=[
-            block,
-            pl.BlockSpec((rows, LANES), lambda c: (0, 0)),
-            pl.BlockSpec((None, rank, width), lambda c: (STEPS - 1, 0, c)),
+        out_shape=(
+            jax.ShapeDtypeStruct((rows, cols), BF16),
+            jax.ShapeDtypeStruct((STEPS, 2, half, cols), F32),
+        ),
+        in_specs=[vmem, vmem, vmem],
+        out_specs=(hbm, hbm),
+        scratch_shapes=[
+            pltpu.VMEM((nown, rows, width), BF16),
+            dma((nown,)),
+            dma,
         ],
-        out_specs=block,
+        compiler_params=pltpu.CompilerParams(vmem_limit_bytes=32 * 1024 * 1024),
         name="update",
     )(current, bt, factors)
-    return (corrected[None], factors[None])
+    return (corrected[None], factors.reshape(1, STEPS, rank, cols))
 
 
 def solution(mesh):

time: 75 us -> 67 us (0.89)
  Pallas kernels: 70.8 us -> 65.2 us
  local copies, waits for them, and re-layouts: 3.28 us -> 0.97 us
    pallas_call x1, Pallas kernels: 8.29 us -> 2.97 us  [shards(): pl.pallas_call(update_kernel, out_shape=(jax.ShapeDtypeStruct((rows, cols...]
    unnamed x9 -> x2, local copies, waits for them, and re-layouts: 3.28 us -> 0.97 us
where the time goes in v2:
time: 67 us; the launch traced here: 66.8 us
  Pallas kernels  65.2 us (97%)
  local copies, waits for them, and re-layouts  0.97 us (1%)
    pallas_call x1, Pallas kernels, shards(): pl.pallas_call(functools.partial(comm_kernel, nrep, nsh, nown), out_shape...  62.3 us
    pallas_call x1, Pallas kernels, shards(): pl.pallas_call(update_kernel, out_shape=(jax.ShapeDtypeStruct((rows, cols...  2.97 us

profile of v2, /device:TPU:0, one launch (start us, length us, event | category | flops | bytes accessed | tf_op | source)
XLA Modules:
  0.0 66.8 jit_solution(14183810681124690919)
XLA Ops:
  0.6 0.0 copy-start
  0.6 1.0 %copy-done = bf16[1,2,16,5120]{3,2,1,0:T(8,128)(2,1)S(1)} copy-done((bf16[1,2,16,5120]{3,2,1,0:T(8,128)(2,1)S(1)}, bf16[1,2,16,5120]{3,2,1,0:T(8,128)(2,1)}, u32[]{:S(2)}) %copy-start) | copy-done | bytes 327704
  1.6 62.3 %rounds.1 = (bf16[512,5120]{1,0:T(8,128)(2,1)S(1)}, f32[2,2,8,5120]{3,2,1,0:T(8,128)S(1)}, bf16[512,128]{1,0:T(8,128)(2,1)S(1)}) custom-call(bf16[512,5120]{1,0:T(8,128)(2,1)} %bitcast.5, bf16[2,16,5120]{2,1,0:T(8,128)(2,1)S(1)} %bitcast.4), custom_call_target="tpu_custom_call" | custom-call | tf_op jit(solution)/shard_map/rounds/pallas_call | solution.py:305
  63.9 3.0 %update.1 = (bf16[512,5120]{1,0:T(8,128)(2,1)}, f32[2,2,8,5120]{3,2,1,0:T(8,128)}) custom-call(bf16[512,5120]{1,0:T(8,128)(2,1)S(1)} %get-tuple-element.7.cur, bf16[512,128]{1,0:T(8,128)(2,1)S(1)} %get-tuple-element.8.bt, f32[2,2,8,5120]{3,2,1,0:T(8,128)S(1)} %get-tuple-element.9.fac), custom_call_target="tpu_custom_call" | custom-call | tf_op jit(solution)/shard_map/update/pallas_call | solution.py:344
Async XLA Ops:
  0.6 1.0 %copy-start = (bf16[1,2,16,5120]{3,2,1,0:T(8,128)(2,1)S(1)}, bf16[1,2,16,5120]{3,2,1,0:T(8,128)(2,1)}, u32[]{:S(2)}) copy-start(bf16[1,2,16,5120]{3,2,1,0:T(8,128)(2,1)} %param.3) | copy-start | bytes 983044

commit v3 on v2

v3 whole, which is shorter than its diff:
```python
import functools
import math

import jax
import jax.numpy as jnp
from jax import lax
from jax.experimental import pallas as pl
from jax.experimental.pallas import tpu as pltpu
from jax.sharding import PartitionSpec as P

STEPS = 2
LANES = 128
VMEM = 67043328
F32 = jnp.float32
BF16 = jnp.bfloat16
NT = (((1,), (1,)), ((), ()))


def split(value):
    high = value.astype(BF16).astype(F32)
    return high, value - high


def stack_left(basis, scale):
    high, low = split(scale * basis)
    rank, rows = basis.shape
    pad = jnp.zeros((LANES - 3 * rank, rows), F32)
    return jnp.concatenate([high, high, low, pad], axis=0).T.astype(BF16)


def stack_right(factor):
    high, low = split(factor)
    rank, cols = factor.shape
    pad = jnp.zeros((LANES - 3 * rank, cols), F32)
    return jnp.concatenate([high, low, high, pad], axis=0).astype(BF16)


def whiten(gram, differ):
    rank = differ.shape[0]
    row = lax.broadcasted_iota(jnp.int32, (rank, 1), 0)
    pivots = jnp.ones((rank, 1), F32)
    for k in range(rank):
        pivot = gram[k : k + 1, k : k + 1]
        pivots = jnp.where(row == k, pivot, pivots)
        if k == rank - 1:
            break
        column = jnp.where(row > k, gram[:, k : k + 1] / pivot, 0.0)
        gram = gram - column * gram[k : k + 1, :]
        differ = differ - column * differ[k : k + 1, :]
    return differ / jnp.sqrt(pivots)


def comm_kernel(
    nrep, nsh, nown,
    w_hbm, starts_hbm, cur, fac, bt_out,
    starts, sk, skin, w1, w1in, cross, crossin, base, basein, gbuf, mbuf, pbuf, pin, psum, rsbuf, bt,
    ld_sem, wm_sem, sk_s, sk_r, w1_s, w1_r, cr_s, cr_r, ba_s, ba_r, g_s, g_r, m_s, m_r,
    p_s, p_r, rs_s, rs_r, ag_s, ag_r, fw_s, fw_r,
):
    rows, cols = cur.shape
    rank = starts.shape[1]
    half_rank = rank // 2
    width = cols // nown
    stride = nsh // nown
    half = nrep // 2
    me_r = lax.axis_index("rep")
    me_s = lax.axis_index("shard")
    me_j = me_s // stride
    bits = (me_r % 2, me_r // half)
    partners = (me_r + 1 - 2 * (me_r % 2), (me_r + half) % nrep)
    signs = tuple((1 - 2 * b).astype(F32) for b in bits)

    def where(j):
        return pl.ds(pl.multiple_of(j * width, LANES), width)

    def load(c):
        return pltpu.make_async_copy(
            w_hbm.at[:, pl.ds(c * width, width)], cur.at[:, pl.ds(c * width, width)], ld_sem.at[c]
        )

    def remote(src, dst, ssem, rsem, rep, shard):
        return pltpu.make_async_remote_copy(
            src_ref=src, dst_ref=dst, send_sem=ssem, recv_sem=rsem,
            device_id={"rep": rep, "shard": shard}, device_id_type=pl.DeviceIdType.MESH,
        )

    def owner(fn, negate=False):
        if stride == 1:
            if not negate:
                fn()
        else:
            here = me_s % stride != 0 if negate else me_s % stride == 0
            pl.when(here)(fn)

    warm = pltpu.make_async_copy(starts_hbm, starts, wm_sem)
    warm.start()
    for c in range(nown):
        load(c).start()

    mate, peer = partners
    barrier = pltpu.get_barrier_semaphore()

    def greet(rep, shard):
        pl.semaphore_signal(
            barrier, inc=1, device_id={"rep": rep, "shard": shard},
            device_id_type=pl.DeviceIdType.MESH,
        )

    for o in range(1, nsh):
        greet(me_r, (me_s + o) % nsh)
    for o in range(nsh):
        greet(peer, (me_s + o) % nsh)
    greet(mate, me_s)

    def pack(square):
        return square[:half_rank] + pltpu.roll(square[half_rank:], rank, 1)

    def unpack(tile):
        return jnp.concatenate([tile, pltpu.roll(tile, LANES - rank, 1)], axis=0)

    def padded(value):
        return jnp.concatenate([value, jnp.zeros((LANES - rank, rows), F32)], axis=0)

    def exact(a, b, dims):
        return lax.dot_general(
            a, b, dims, precision=lax.Precision.HIGHEST, preferred_element_type=F32
        )

    def slots(buf):
        total = buf[0]
        for s in range(1, nsh):
            total = total + buf[s]
        return total

    both = jnp.zeros((STEPS * rank, rows), F32)
    warm.wait()
    w1[...] = starts[1].astype(F32)
    for c in range(nown):
        load(c).wait()
        part = pl.ds(c * width, width)
        both = both + lax.dot_general(
            jnp.concatenate([starts[0, :, part], starts[1, :, part]], axis=0),
            cur[:, part], NT, preferred_element_type=F32,
        )
    sketches = (both[:rank], both[rank:])
    pl.semaphore_wait(barrier, 2 * nsh)

    def swap(k):
        return remote(sk.at[k], skin.at[k], sk_s.at[k], sk_r.at[k], partners[k], me_s)

    give_starts = remote(w1, w1in, w1_s, w1_r, mate, me_s)
    give_cross = remote(cross, crossin, cr_s, cr_r, mate, me_s)
    give_base = remote(base, basein, ba_s, ba_r, peer, me_s)
    for k in range(STEPS):
        sk[k] = sketches[k]
        swap(k).start()
    give_starts.start()

    def gsend(k, o):
        other = (me_s + o) % nsh
        return remote(
            gbuf.at[k, me_s], gbuf.at[k, me_s], g_s.at[k, other], g_r.at[k, me_s], me_r, other
        )

    def gwait(k, o):
        other = (me_s + o) % nsh
        return remote(
            gbuf.at[k, other], gbuf.at[k, other], g_s.at[k, other], g_r.at[k, other], me_r, other
        )

    def msend(g, o):
        other = (me_s + o) % nsh
        return remote(
            mbuf.at[0, me_s], mbuf.at[g, me_s], m_s.at[g, other], m_r.at[g, me_s],
            (me_r, peer)[g], other,
        )

    def mwait(g, o):
        other = (me_s + o) % nsh
        return remote(
            mbuf.at[g, other], mbuf.at[g, other], m_s.at[g, other], m_r.at[g, other],
            (me_r, peer)[g], other,
        )

    def psend(k, j):
        return remote(
            pbuf.at[k, 1 - bits[k], :, where(j)], pin.at[k, j], p_s.at[k, j], p_r.at[k, j],
            partners[k], me_s,
        )

    def rsend(k, j):
        return remote(
            psum.at[k, j], rsbuf.at[k, me_s], rs_s.at[k, j], rs_r.at[k, me_s], me_r, j * stride
        )

    def rwait(k, o):
        other = (me_s + o) % nsh
        return remote(
            rsbuf.at[k, other], rsbuf.at[k, other], rs_s.at[k, 0], rs_r.at[k, other], me_r, other
        )

    def asend(k, o):
        other = (me_s + o) % nsh
        piece = fac.at[k, bits[k], :, where(me_j)]
        return remote(piece, piece, ag_s.at[k, other], ag_r.at[k, me_j], me_r, other)

    def await_piece(k, j):
        piece = fac.at[k, bits[k], :, where(j)]
        return remote(piece, piece, ag_s.at[k, 0], ag_r.at[k, j], me_r, j * stride)

    def fsend(k, j):
        piece = fac.at[k, bits[k], :, where(j)]
        return remote(piece, piece, fw_s.at[k, j], fw_r.at[k, j], partners[k], me_s)

    def fwait(k, j):
        piece = fac.at[k, 1 - bits[k], :, where(j)]
        return remote(piece, piece, fw_s.at[k, j], fw_r.at[k, j], partners[k], me_s)

    order = [(me_j + 1 + i) % nown for i in range(nown)]

    def send_gram(k, differ):
        gbuf[k, me_s] = pack(exact(differ, padded(differ), NT))
        for o in range(1, nsh):
            gsend(k, o).start()

    def finish_basis(k, differ):
        for o in range(1, nsh):
            gwait(k, o).wait_recv()
        return whiten(unpack(slots(gbuf.at[k])), differ)

    def project(k, basis_half, j):
        product = signs[k] * jnp.dot(
            basis_half, cur[:, where(j)], preferred_element_type=F32
        )
        pbuf[k, 0, :, where(j)] = product[:half_rank]
        pbuf[k, 1, :, where(j)] = product[half_rank:]
        psend(k, j).start()

    def pass_on(k, j):
        psend(k, j).wait_recv()
        psum[k, j] = pbuf[k, bits[k], :, where(j)] + pin[k, j]

    def pass_out(k, i):
        pass_on(k, order[i])
        if i < nown - 1:
            rsend(k, order[i]).start()
        else:
            owner(lambda: rsend(k, order[i]).start(), negate=True)

    def reduce_and_send(k):
        def mine():
            for o in range(1, nsh):
                rwait(k, o).wait_recv()
            total = psum[k, me_j]
            for o in range(1, nsh):
                total = total + rsbuf[k, (me_s + o) % nsh]
            fac[k, bits[k], :, where(me_j)] = total
            for o in range(1, nsh):
                asend(k, o).start()

        owner(mine)

    def relay(k, i):
        j = (me_j + i) % nown
        if i:
            await_piece(k, j).wait_recv()
        else:
            owner(lambda: await_piece(k, j).wait_recv(), negate=True)
        fsend(k, j).start()

    lag = 2
    swap(0).wait_recv()
    differ = signs[0] * (sketches[0] - skin[0])
    send_gram(0, differ)
    give_starts.wait_recv()
    other = jnp.zeros((rank, rows), F32)
    for c in range(nown):
        part = pl.ds(c * width, width)
        other = other + lax.dot_general(
            w1in[:, part].astype(BF16), cur[:, part], NT, preferred_element_type=F32
        )
    cross[...] = other
    give_cross.start()
    basis = finish_basis(0, differ)
    base[...] = basis
    give_base.start()
    basis_half = basis.astype(BF16)
    give_cross.wait_recv()
    mbuf[0, me_s] = pack(
        signs[0] * exact(sketches[1] - crossin[...], padded(basis_half.astype(F32)), NT)
    )
    for o in range(nsh):
        if o:
            msend(0, o).start()
        msend(1, o).start()
    for i in range(nown):
        project(0, basis_half, order[i])
        if i >= lag:
            pass_out(0, i - lag)
    for i in range(max(nown - lag, 0), nown):
        pass_out(0, i)
    bt[0] = stack_left(basis, -0.5 * signs[0])
    swap(1).wait_recv()
    give_base.wait_recv()
    for o in range(nsh):
        if o:
            mwait(0, o).wait_recv()
        mwait(1, o).wait_recv()
    fix = -0.5 * signs[0]

    def moved(sketch, group, base_rows):
        return sketch + fix * exact(
            unpack(slots(mbuf.at[group])), padded(base_rows), (((1,), (0,)), ((), ()))
        )

    differ = signs[1] * (moved(sketches[1], 0, basis) - moved(skin[1], 1, basein[...]))
    send_gram(1, differ)
    reduce_and_send(0)
    basis = finish_basis(1, differ)
    basis_half = basis.astype(BF16)

    def update(i):
        j = (me_j + i) % nown
        fwait(0, j).wait_recv()
        piece = jnp.concatenate([fac[0, 0, :, where(j)], fac[0, 1, :, where(j)]], axis=0)
        change = jnp.dot(bt[0], stack_right(piece), preferred_element_type=F32)
        cur[:, where(j)] = (cur[:, where(j)].astype(F32) + change).astype(BF16)
        project(1, basis_half, j)

    seq = list(range(1, nown)) + [0]
    relay(0, 0)
    for n in range(1, nown):
        relay(0, n)
    bt_out[...] = stack_left(basis, -0.5 * signs[1])
    for n in range(nown):
        update(seq[n])
        if n >= lag:
            pass_out(1, n - lag)
    for i in range(max(nown - lag, 0), nown):
        pass_out(1, i)
    reduce_and_send(1)
    for n in range(nown):
        relay(1, n)
    for n in range(nown):
        fwait(1, (me_j + n) % nown).wait_recv()

    give_starts.wait_send()
    give_cross.wait_send()
    give_base.wait_send()
    for o in range(nsh):
        if o:
            msend(0, o).wait_send()
        msend(1, o).wait_send()
    for k in range(STEPS):
        swap(k).wait_send()
        for o in range(1, nsh):
            gsend(k, o).wait_send()
        for i in range(nown):
            psend(k, order[i]).wait_send()
            fsend(k, order[i]).wait_send()
            if i < nown - 1:
                rsend(k, order[i]).wait_send()

    def sent_all():
        for k in range(STEPS):
            for o in range(1, nsh):
                asend(k, o).wait_send()

    def sent_own():
        for k in range(STEPS):
            rsend(k, me_j).wait_send()

    owner(sent_all)
    owner(sent_own, negate=True)


def update_kernel(cur, bt, fac, cur_out, fac_out, fresh, st_sem, fo_sem):
    pieces, _, width = fresh.shape
    factors = pltpu.make_async_copy(fac, fac_out, fo_sem)
    factors.start()

    def store(c):
        return pltpu.make_async_copy(
            fresh.at[c], cur_out.at[:, pl.ds(c * width, width)], st_sem.at[c]
        )

    for c in range(pieces):
        part = pl.ds(c * width, width)
        piece = jnp.concatenate([fac[STEPS - 1, 0, :, part], fac[STEPS - 1, 1, :, part]], axis=0)
        change = jnp.dot(bt[...], stack_right(piece), preferred_element_type=F32)
        fresh[c] = (cur[:, part].astype(F32) + change).astype(BF16)
        store(c).start()
    factors.wait()
    for c in range(pieces):
        store(c).wait()


def shards(weights, warm_start):
    nrep, nsh = lax.axis_size("rep"), lax.axis_size("shard")
    _, rows, cols = weights.shape
    rank = warm_start.shape[2]
    half = rank // 2
    nown = math.gcd(cols // LANES, nsh)
    width = cols // nown
    dma = pltpu.SemaphoreType.DMA
    held = 2 * rows * cols + 4 * STEPS * rank * cols + 2 * rows * LANES + 13000 * 1024
    hbm = pl.BlockSpec(memory_space=pltpu.HBM)
    vmem = pl.BlockSpec(memory_space=pltpu.VMEM)
    current, factors, bt = pl.pallas_call(
        functools.partial(comm_kernel, nrep, nsh, nown),
        out_shape=(
            jax.ShapeDtypeStruct((rows, cols), BF16),
            jax.ShapeDtypeStruct((STEPS, 2, half, cols), F32),
            jax.ShapeDtypeStruct((rows, LANES), BF16),
        ),
        in_specs=[hbm, hbm],
        out_specs=(vmem, vmem, vmem),
        scratch_shapes=[
            pltpu.VMEM(warm_start.shape[1:], BF16),
            pltpu.VMEM((STEPS, rank, rows), F32),
            pltpu.VMEM((STEPS, rank, rows), F32),
            pltpu.VMEM((rank, cols), F32),
            pltpu.VMEM((rank, cols), F32),
            pltpu.VMEM((rank, rows), F32),
            pltpu.VMEM((rank, rows), F32),
            pltpu.VMEM((rank, rows), F32),
            pltpu.VMEM((rank, rows), F32),
            pltpu.VMEM((STEPS, nsh, half, LANES), F32),
            pltpu.VMEM((STEPS, nsh, half, LANES), F32),
            pltpu.VMEM((STEPS, 2, half, cols), F32),
            pltpu.VMEM((STEPS, nown, half, width), F32),
            pltpu.VMEM((STEPS, nown, half, width), F32),
            pltpu.VMEM((STEPS, nsh, half, width), F32),
            pltpu.VMEM((1, rows, LANES), BF16),
            dma((nown,)),
            dma,
            dma((STEPS,)),
            dma((STEPS,)),
            dma,
            dma,
            dma,
            dma,
            dma,
            dma,
            dma((STEPS, nsh)),
            dma((STEPS, nsh)),
            dma((STEPS, nsh)),
            dma((STEPS, nsh)),
            dma((STEPS, nown)),
            dma((STEPS, nown)),
            dma((STEPS, nown)),
            dma((STEPS, nsh)),
            dma((STEPS, nsh)),
            dma((STEPS, nown)),
            dma((STEPS, nown)),
            dma((STEPS, nown)),
        ],
        compiler_params=pltpu.CompilerParams(
            collective_id=0, has_side_effects=True, vmem_limit_bytes=VMEM - held
        ),
        name="rounds",
    )(weights[0], warm_start[0])
    corrected, factors = pl.pallas_call(
        update_kernel,
        out_shape=(
            jax.ShapeDtypeStruct((rows, cols), BF16),
            jax.ShapeDtypeStruct((STEPS, 2, half, cols), F32),
        ),
        in_specs=[vmem, vmem, vmem],
        out_specs=(hbm, hbm),
        scratch_shapes=[
            pltpu.VMEM((nown, rows, width), BF16),
            dma((nown,)),
            dma,
        ],
        compiler_params=pltpu.CompilerParams(vmem_limit_bytes=32 * 1024 * 1024),
        name="update",
    )(current, bt, factors)
    return (corrected[None], factors.reshape(1, STEPS, rank, cols))


def solution(mesh):
    placed = (P("rep", "shard", None), P("rep", None, None, None))
    return jax.shard_map(
        shards,
        mesh=mesh,
        in_specs=placed,
        out_specs=(P("rep", "shard", None), P("rep", None, None, None)),
        check_vma=False,
    )
```

time: 67 us -> 54.1 us (0.81)
  Pallas kernels: 65.2 us -> 52.3 us
    pallas_call x1, Pallas kernels: 62.3 us -> 49.4 us  [shards(): pl.pallas_call(functools.partial(comm_kernel, nrep, nsh, nown), out_shape...]
where the time goes in v3:
time: 54.1 us; the launch traced here: 54 us
  Pallas kernels  52.3 us (97%)
  local copies, waits for them, and re-layouts  0.97 us (2%)
  between operations  0.65 us (1%)
    pallas_call x1, Pallas kernels, shards(): pl.pallas_call(functools.partial(comm_kernel, nrep, nsh, nown), out_shape...  49.4 us
    pallas_call x1, Pallas kernels, shards(): pl.pallas_call(update_kernel, out_shape=(jax.ShapeDtypeStruct((rows, cols...  2.96 us

profile of v3, /device:TPU:0, one launch (start us, length us, event | category | flops | bytes accessed | tf_op | source)
XLA Modules:
  0.0 54.0 jit_solution(15750149209625886220)
XLA Ops:
  0.6 0.0 copy-start
  0.6 1.0 %copy-done = bf16[1,2,16,5120]{3,2,1,0:T(8,128)(2,1)S(1)} copy-done((bf16[1,2,16,5120]{3,2,1,0:T(8,128)(2,1)S(1)}, bf16[1,2,16,5120]{3,2,1,0:T(8,128)(2,1)}, u32[]{:S(2)}) %copy-start) | copy-done | bytes 327704
  1.6 49.4 %rounds.1 = (bf16[512,5120]{1,0:T(8,128)(2,1)S(1)}, f32[2,2,8,5120]{3,2,1,0:T(8,128)S(1)}, bf16[512,128]{1,0:T(8,128)(2,1)S(1)}) custom-call(bf16[512,5120]{1,0:T(8,128)(2,1)} %bitcast.5, bf16[2,16,5120]{2,1,0:T(8,128)(2,1)S(1)} %bitcast.4), custom_call_target="tpu_custom_call" | custom-call | tf_op jit(solution)/shard_map/rounds/pallas_call | solution.py:409
  51.0 3.0 %update.1 = (bf16[512,5120]{1,0:T(8,128)(2,1)}, f32[2,2,8,5120]{3,2,1,0:T(8,128)}) custom-call(bf16[512,5120]{1,0:T(8,128)(2,1)S(1)} %get-tuple-element.7.cur, bf16[512,128]{1,0:T(8,128)(2,1)S(1)} %get-tuple-element.8.bt, f32[2,2,8,5120]{3,2,1,0:T(8,128)S(1)} %get-tuple-element.9.fac), custom_call_target="tpu_custom_call" | custom-call | tf_op jit(solution)/shard_map/update/pallas_call | solution.py:463
Async XLA Ops:
  0.6 1.0 %copy-start = (bf16[1,2,16,5120]{3,2,1,0:T(8,128)(2,1)S(1)}, bf16[1,2,16,5120]{3,2,1,0:T(8,128)(2,1)}, u32[]{:S(2)}) copy-start(bf16[1,2,16,5120]{3,2,1,0:T(8,128)(2,1)} %param.3) | copy-start | bytes 983044

commit v4 on v3

--- a/solution.py
+++ b/solution.py
@@ -53,8 +53,8 @@
 def comm_kernel(
     nrep, nsh, nown,
     w_hbm, starts_hbm, cur, fac, bt_out,
-    starts, sk, skin, w1, w1in, cross, crossin, base, basein, gbuf, mbuf, pbuf, pin, psum, rsbuf, bt,
-    ld_sem, wm_sem, sk_s, sk_r, w1_s, w1_r, cr_s, cr_r, ba_s, ba_r, g_s, g_r, m_s, m_r,
+    starts, sk, skin, w1, w1in, cross, crossin, base, basein, gbuf, mbuf, qbuf, peerfac, pbuf, pin, psum, rsbuf, bt,
+    ld_sem, wm_sem, sk_s, sk_r, w1_s, w1_r, cr_s, cr_r, ba_s, ba_r, g_s, g_r, m_s, m_r, q_s, q_r, pf_s, pf_r,
     p_s, p_r, rs_s, rs_r, ag_s, ag_r, fw_s, fw_r,
 ):
     rows, cols = cur.shape
@@ -168,19 +168,26 @@
             gbuf.at[k, other], gbuf.at[k, other], g_s.at[k, other], g_r.at[k, other], me_r, other
         )
 
-    def msend(g, o):
-        other = (me_s + o) % nsh
-        return remote(
-            mbuf.at[0, me_s], mbuf.at[g, me_s], m_s.at[g, other], m_r.at[g, me_s],
-            (me_r, peer)[g], other,
-        )
-
-    def mwait(g, o):
-        other = (me_s + o) % nsh
-        return remote(
-            mbuf.at[g, other], mbuf.at[g, other], m_s.at[g, other], m_r.at[g, other],
-            (me_r, peer)[g], other,
-        )
+    def small(buf, ssem, rsem):
+        def send(g, o):
+            other = (me_s + o) % nsh
+            return remote(
+                buf.at[0, me_s], buf.at[g, me_s], ssem.at[g, other], rsem.at[g, me_s],
+                (me_r, peer)[g], other,
+            )
+
+        def arrival(g, o):
+            other = (me_s + o) % nsh
+            return remote(
+                buf.at[g, other], buf.at[g, other], ssem.at[g, other], rsem.at[g, other],
+                (me_r, peer)[g], other,
+            )
+
+        return send, arrival
+
+    pairs = [(g, o) for o in range(nsh) for g in range(2) if g or o]
+    msend, mwait = small(mbuf, m_s, m_r)
+    qsend, qwait = small(qbuf, q_s, q_r)
 
     def psend(k, j):
         return remote(
@@ -247,15 +254,17 @@
         else:
             owner(lambda: rsend(k, order[i]).start(), negate=True)
 
-    def reduce_and_send(k):
+    def reduce_and_send(k, extra=None):
         def mine():
             for o in range(1, nsh):
                 rwait(k, o).wait_recv()
             total = psum[k, me_j]
             for o in range(1, nsh):
                 total = total + rsbuf[k, (me_s + o) % nsh]
+            if extra is not None:
+                total = total + extra
             fac[k, bits[k], :, where(me_j)] = total
-            for o in range(1, nsh):
+            for o in range(nsh - 1, 0, -1):
                 asend(k, o).start()
 
         owner(mine)
@@ -289,10 +298,8 @@
     mbuf[0, me_s] = pack(
         signs[0] * exact(sketches[1] - crossin[...], padded(basis_half.astype(F32)), NT)
     )
-    for o in range(nsh):
-        if o:
-            msend(0, o).start()
-        msend(1, o).start()
+    for g, o in pairs:
+        msend(g, o).start()
     for i in range(nown):
         project(0, basis_half, order[i])
         if i >= lag:
@@ -302,10 +309,8 @@
     bt[0] = stack_left(basis, -0.5 * signs[0])
     swap(1).wait_recv()
     give_base.wait_recv()
-    for o in range(nsh):
-        if o:
-            mwait(0, o).wait_recv()
-        mwait(1, o).wait_recv()
+    for g, o in pairs:
+        mwait(g, o).wait_recv()
     fix = -0.5 * signs[0]
 
     def moved(sketch, group, base_rows):
@@ -316,29 +321,50 @@
     differ = signs[1] * (moved(sketches[1], 0, basis) - moved(skin[1], 1, basein[...]))
     send_gram(1, differ)
     reduce_and_send(0)
+    relay(0, 0)
     basis = finish_basis(1, differ)
     basis_half = basis.astype(BF16)
-
-    def update(i):
-        j = (me_j + i) % nown
-        fwait(0, j).wait_recv()
+    qbuf[0, me_s] = pack(exact(basis_half.astype(F32), padded(base[...]), NT))
+    for g, o in pairs:
+        qsend(g, o).start()
+    for i in range(nown):
+        project(1, basis_half, order[i])
+        if i >= lag:
+            pass_out(1, i - lag)
+    for i in range(max(nown - lag, 0), nown):
+        pass_out(1, i)
+    for n in range(1, nown):
+        relay(0, n)
+    fwait(0, me_j).wait_recv()
+    give_factor = remote(
+        fac.at[0, :, :, where(me_j)], peerfac, pf_s, pf_r, peer, me_s
+    )
+    give_factor.start()
+    bt_out[...] = stack_left(basis, -0.5 * signs[1])
+
+    def update(j):
         piece = jnp.concatenate([fac[0, 0, :, where(j)], fac[0, 1, :, where(j)]], axis=0)
         change = jnp.dot(bt[0], stack_right(piece), preferred_element_type=F32)
         cur[:, where(j)] = (cur[:, where(j)].astype(F32) + change).astype(BF16)
-        project(1, basis_half, j)
-
-    seq = list(range(1, nown)) + [0]
-    relay(0, 0)
+
+    update(me_j)
     for n in range(1, nown):
-        relay(0, n)
-    bt_out[...] = stack_left(basis, -0.5 * signs[1])
-    for n in range(nown):
-        update(seq[n])
-        if n >= lag:
-            pass_out(1, n - lag)
-    for i in range(max(nown - lag, 0), nown):
-        pass_out(1, i)
-    reduce_and_send(1)
+        j = (me_j + n) % nown
+        fwait(0, j).wait_recv()
+        update(j)
+    for g, o in pairs:
+        qwait(g, o).wait_recv()
+    give_factor.wait_recv()
+
+    def shift(group, halves):
+        piece = jnp.concatenate(
+            [halves[0], halves[1], jnp.zeros((LANES - rank, width), F32)], axis=0
+        )
+        return exact(unpack(slots(qbuf.at[group])), piece, (((1,), (0,)), ((), ())))
+
+    own = (fac[0, 0, :, where(me_j)], fac[0, 1, :, where(me_j)])
+    shifted = fix * signs[1] * (shift(0, own) - shift(1, (peerfac[0], peerfac[1])))
+    reduce_and_send(1, jnp.where(bits[1] == 0, shifted[:half_rank], shifted[half_rank:]))
     for n in range(nown):
         relay(1, n)
     for n in range(nown):
@@ -347,10 +373,10 @@
     give_starts.wait_send()
     give_cross.wait_send()
     give_base.wait_send()
-    for o in range(nsh):
-        if o:
-            msend(0, o).wait_send()
-        msend(1, o).wait_send()
+    give_factor.wait_send()
+    for g, o in pairs:
+        msend(g, o).wait_send()
+        qsend(g, o).wait_send()
     for k in range(STEPS):
         swap(k).wait_send()
         for o in range(1, nsh):
@@ -426,7 +452,9 @@
             pltpu.VMEM((rank, rows), F32),
             pltpu.VMEM((rank, rows), F32),
             pltpu.VMEM((STEPS, nsh, half, LANES), F32),
-            pltpu.VMEM((STEPS, nsh, half, LANES), F32),
+            pltpu.VMEM((2, nsh, half, LANES), F32),
+            pltpu.VMEM((2, nsh, half, LANES), F32),
+            pltpu.VMEM((2, half, width), F32),
             pltpu.VMEM((STEPS, 2, half, cols), F32),
             pltpu.VMEM((STEPS, nown, half, width), F32),
             pltpu.VMEM((STEPS, nown, half, width), F32),
@@ -444,8 +472,12 @@
             dma,
             dma((STEPS, nsh)),
             dma((STEPS, nsh)),
-            dma((STEPS, nsh)),
-            dma((STEPS, nsh)),
+            dma((2, nsh)),
+            dma((2, nsh)),
+            dma((2, nsh)),
+            dma((2, nsh)),
+            dma,
+            dma,
             dma((STEPS, nown)),
             dma((STEPS, nown)),
             dma((STEPS, nown)),

time: 54.1 us -> 54.4 us (level)
  no operation moved by 1% of the time
where the time goes in v4:
time: 54.4 us; the launch traced here: 54.3 us
  Pallas kernels  52.7 us (97%)
  local copies, waits for them, and re-layouts  0.97 us (2%)
  between operations  0.65 us (1%)
    pallas_call x1, Pallas kernels, shards(): pl.pallas_call(functools.partial(comm_kernel, nrep, nsh, nown), out_shape...  49.7 us
    pallas_call x1, Pallas kernels, shards(): pl.pallas_call(update_kernel, out_shape=(jax.ShapeDtypeStruct((rows, cols...  2.96 us

profile of v4, /device:TPU:0, one launch (start us, length us, event | category | flops | bytes accessed | tf_op | source)
XLA Modules:
  0.0 54.3 jit_solution(15668728221873740199)
XLA Ops:
  0.6 0.0 copy-start
  0.6 1.0 %copy-done = bf16[1,2,16,5120]{3,2,1,0:T(8,128)(2,1)S(1)} copy-done((bf16[1,2,16,5120]{3,2,1,0:T(8,128)(2,1)S(1)}, bf16[1,2,16,5120]{3,2,1,0:T(8,128)(2,1)}, u32[]{:S(2)}) %copy-start) | copy-done | bytes 327704
  1.6 49.7 %rounds.1 = (bf16[512,5120]{1,0:T(8,128)(2,1)S(1)}, f32[2,2,8,5120]{3,2,1,0:T(8,128)S(1)}, bf16[512,128]{1,0:T(8,128)(2,1)S(1)}) custom-call(bf16[512,5120]{1,0:T(8,128)(2,1)} %bitcast.5, bf16[2,16,5120]{2,1,0:T(8,128)(2,1)S(1)} %bitcast.4), custom_call_target="tpu_custom_call" | custom-call | tf_op jit(solution)/shard_map/rounds/pallas_call | solution.py:435
  51.3 3.0 %update.1 = (bf16[512,5120]{1,0:T(8,128)(2,1)}, f32[2,2,8,5120]{3,2,1,0:T(8,128)}) custom-call(bf16[512,5120]{1,0:T(8,128)(2,1)S(1)} %get-tuple-element.7.cur, bf16[512,128]{1,0:T(8,128)(2,1)S(1)} %get-tuple-element.8.bt, f32[2,2,8,5120]{3,2,1,0:T(8,128)S(1)} %get-tuple-element.9.fac), custom_call_target="tpu_custom_call" | custom-call | tf_op jit(solution)/shard_map/update/pallas_call | solution.py:495
Async XLA Ops:
  0.6 1.0 %copy-start = (bf16[1,2,16,5120]{3,2,1,0:T(8,128)(2,1)S(1)}, bf16[1,2,16,5120]{3,2,1,0:T(8,128)(2,1)}, u32[]{:S(2)}) copy-start(bf16[1,2,16,5120]{3,2,1,0:T(8,128)(2,1)} %param.3) | copy-start | bytes 983044

commit v5 on v3

--- a/solution.py
+++ b/solution.py
@@ -255,7 +255,7 @@
             for o in range(1, nsh):
                 total = total + rsbuf[k, (me_s + o) % nsh]
             fac[k, bits[k], :, where(me_j)] = total
-            for o in range(1, nsh):
+            for o in range(nsh - 1, 0, -1):
                 asend(k, o).start()
 
         owner(mine)

time: 54.1 us -> 55.7 us (1.030)
  Pallas kernels: 52.3 us -> 54 us
    pallas_call x1, Pallas kernels: 49.4 us -> 51 us  [shards(): pl.pallas_call(functools.partial(comm_kernel, nrep, nsh, nown), out_shape...]
where the time goes in v5:
time: 55.7 us; the launch traced here: 55.6 us
  Pallas kernels  54 us (97%)
  local copies, waits for them, and re-layouts  0.97 us (2%)
  between operations  0.65 us (1%)
    pallas_call x1, Pallas kernels, shards(): pl.pallas_call(functools.partial(comm_kernel, nrep, nsh, nown), out_shape...  51 us
    pallas_call x1, Pallas kernels, shards(): pl.pallas_call(update_kernel, out_shape=(jax.ShapeDtypeStruct((rows, cols...  2.97 us

profile of v5, /device:TPU:0, one launch (start us, length us, event | category | flops | bytes accessed | tf_op | source)
XLA Modules:
  0.0 55.6 jit_solution(6721019562216884423)
XLA Ops:
  0.6 0.0 copy-start
  0.6 1.0 %copy-done = bf16[1,2,16,5120]{3,2,1,0:T(8,128)(2,1)S(1)} copy-done((bf16[1,2,16,5120]{3,2,1,0:T(8,128)(2,1)S(1)}, bf16[1,2,16,5120]{3,2,1,0:T(8,128)(2,1)}, u32[]{:S(2)}) %copy-start) | copy-done | bytes 327704
  1.6 51.0 %rounds.1 = (bf16[512,5120]{1,0:T(8,128)(2,1)S(1)}, f32[2,2,8,5120]{3,2,1,0:T(8,128)S(1)}, bf16[512,128]{1,0:T(8,128)(2,1)S(1)}) custom-call(bf16[512,5120]{1,0:T(8,128)(2,1)} %bitcast.5, bf16[2,16,5120]{2,1,0:T(8,128)(2,1)S(1)} %bitcast.4), custom_call_target="tpu_custom_call" | custom-call | tf_op jit(solution)/shard_map/rounds/pallas_call | solution.py:409
  52.6 3.0 %update.1 = (bf16[512,5120]{1,0:T(8,128)(2,1)}, f32[2,2,8,5120]{3,2,1,0:T(8,128)}) custom-call(bf16[512,5120]{1,0:T(8,128)(2,1)S(1)} %get-tuple-element.7.cur, bf16[512,128]{1,0:T(8,128)(2,1)S(1)} %get-tuple-element.8.bt, f32[2,2,8,5120]{3,2,1,0:T(8,128)S(1)} %get-tuple-element.9.fac), custom_call_target="tpu_custom_call" | custom-call | tf_op jit(solution)/shard_map/update/pallas_call | solution.py:463
Async XLA Ops:
  0.6 1.0 %copy-start = (bf16[1,2,16,5120]{3,2,1,0:T(8,128)(2,1)S(1)}, bf16[1,2,16,5120]{3,2,1,0:T(8,128)(2,1)}, u32[]{:S(2)}) copy-start(bf16[1,2,16,5120]{3,2,1,0:T(8,128)(2,1)} %param.3) | copy-start | bytes 983044
